TPU v7x, 32 devices: a whole 2x2x4 slice. The times are simulated.
32 devices in a mesh: dp: 8 (over z, x), ctx: 4 (over y, core).
Axes of the slice: x: 2, y: 2, z: 4, core: 2. Of those that a mesh axis runs over, the one named last changes fastest.
Arguments:
- tokens: bfloat16 [32, 2560, 1280], P('dp', 'ctx'), may hold values from -64 to 64
- router: bfloat16 [1280, 64], replicated, may hold values from -1 to 1
- expert_up: bfloat16 [32, 1280, 2560], P(('dp', 'ctx')), may hold values from -0.5 to 0.5
- expert_down: bfloat16 [32, 2560, 1280], P(('dp', 'ctx')), may hold values from -0.25 to 0.25
Outputs:
- mixed: bfloat16 [32, 2560, 1280], P('dp', 'ctx')
All inputs are finite; a program needn't handle non-finite values.
Results may differ from a plain program's by a relative error of at most 0.015.
Values may be sent and summed in bfloat16 or wider, within the bound.
A program may use at most 128 MiB of HBM per device.

v0:
```python
import jax
import jax.numpy as jnp
from jax import lax
from jax.sharding import PartitionSpec as P


def merged(x, axis, combine):
    everything = jax.tree.map(lambda part: lax.all_gather(part, axis), x)
    initial = jax.tree.map(lambda part: part[0], everything)

    def step(k, so_far):
        return combine(so_far, jax.tree.map(lambda part: part[k], everything))

    return lax.fori_loop(1, lax.axis_size(axis), step, initial)


def merge_stats(earlier, later):
    highest = jnp.maximum(earlier[0], later[0])
    return (
        highest,
        earlier[1] * jnp.exp(earlier[0] - highest) + later[1] * jnp.exp(later[0] - highest),
    )


def expert_rows(grouped, up_matrix, down_matrix):
    feature = grouped.shape[-1]
    flat = grouped.reshape(-1, feature)
    hidden = jax.nn.gelu(
        jnp.dot(flat, up_matrix, preferred_element_type=jnp.float32), approximate=False
    ).astype(jnp.bfloat16)
    produced = jnp.dot(hidden, down_matrix, preferred_element_type=jnp.float32).astype(jnp.bfloat16)
    return produced.reshape(grouped.shape)


def shards(tokens, router, expert_up, expert_down):
    clip_dev, tok_dev, feature = tokens.shape
    dp_size = lax.axis_size("dp")
    ctx_size = lax.axis_size("ctx")
    slot_total = router.shape[1]
    per_expert = slot_total // (dp_size * ctx_size)
    ordered = (
        router.reshape(feature, dp_size, ctx_size, per_expert)
        .transpose(0, 2, 1, 3)
        .reshape(feature, slot_total)
    )
    logits = jnp.einsum("ctd,dj->ctj", tokens, ordered, preferred_element_type=jnp.float32)
    local_max = jnp.max(logits, axis=1)
    exponent = jnp.exp(logits - local_max[:, None, :])
    column_max, column_sum = merged((local_max, jnp.sum(exponent, axis=1)), "ctx", merge_stats)
    exponent = exponent * jnp.exp(local_max - column_max)[:, None, :]
    dispatch = (exponent / column_sum[:, None, :]).astype(jnp.bfloat16)
    row_max = jnp.max(logits, axis=2)
    row_exp = jnp.exp(logits - row_max[:, :, None])
    combine = (row_exp / jnp.sum(row_exp, axis=2)[:, :, None]).astype(jnp.bfloat16)
    up_matrix = expert_up[0]
    down_matrix = expert_down[0]
    split_dispatch = dispatch.reshape(clip_dev, tok_dev, ctx_size, dp_size, per_expert)
    partial_value = jnp.einsum(
        "ctabs,ctd->cbasd", split_dispatch, tokens, preferred_element_type=jnp.float32
    ).astype(jnp.bfloat16)
    grouped = partial_value.reshape(clip_dev, dp_size * ctx_size, per_expert, feature)
    received = lax.all_to_all(grouped, ("dp", "ctx"), split_axis=1, concat_axis=1, tiled=True)
    amount = received.shape[0]
    blocks = received.astype(jnp.float32).reshape(amount, dp_size, ctx_size, per_expert, feature)
    results = expert_rows(jnp.sum(blocks, axis=2).astype(jnp.bfloat16), up_matrix, down_matrix)
    returned = lax.all_to_all(results, "dp", split_axis=1, concat_axis=1, tiled=True)
    returned = returned.reshape(clip_dev, dp_size * per_expert, feature)
    mixed = jnp.einsum(
        "ctj,cjd->ctd",
        combine,
        lax.all_gather(returned, "ctx", axis=1, tiled=True),
        preferred_element_type=jnp.float32,
    )
    return mixed.astype(jnp.bfloat16)


def solution(mesh):
    in_specs = (
        P("dp", "ctx", None),
        P(),
        P(("dp", "ctx"), None, None),
        P(("dp", "ctx"), None, None),
    )
    out_specs = P("dp", "ctx", None)
    return jax.shard_map(shards, mesh=mesh, in_specs=in_specs, out_specs=out_specs, check_vma=False)
```

profile of v0, /device:TPU:0, one launch (start us, length us, event | category | flops | bytes accessed | tf_op | source)
XLA Modules:
  0.0 80.9 jit_solution(9452041933624076778)
XLA Ops:
  0.0 1.0 %reshape.38 = bf16[1280,8,4,2]{0,3,2,1:T(2,128)(2,1)S(1)} reshape(bf16[1280,64]{0,1:T(8,128)(2,1)} %param.7) | data formatting | bytes 327680 | tf_op jit(solution)/shard_map/reshape | solution.py:42
  1.0 0.1 copy.22
  1.1 0.1 reshape.60
  1.2 5.0 %fusion.98 = (f32[4,64]{1,0:T(4,128)S(1)}, f32[4,640,64]{1,2,0:T(8,128)S(1)}) fusion(bf16[4,640,1280]{2,1,0:T(8,128)(2,1)} %param.6, bf16[1280,64,1]{0,1,2:T(8,128)(2,1)S(1)} %reshape.60), kind=kOutput, calls=%fused_computation.108 | convolution fusion | flops 419593984 | bytes 7373824 | tf_op jit(solution)/shard_map/ctd,dj->ctj/dot_general | solution.py:46
  6.2 0.3 fusion.34
  6.5 6.2 %all-gather.3 = f32[4,4,64]{2,1,0:T(4,128)S(1)} all-gather(f32[1,4,64]{2,1,0:T(4,128)S(1)} %bitcast.63), channel_id=3, replica_groups=mesh['dp'=8,'ctx'=4] {'ctx'}, dimensions={0}, use_global_device_ids=true | all-gather | bytes 5120 | tf_op jit(solution)/shard_map/all_gather | solution.py:8
  12.7 5.5 %all-gather.2 = f32[4,4,64]{2,1,0:T(4,128)S(1)} all-gather(f32[1,4,64]{2,1,0:T(4,128)S(1)} %bitcast.62), channel_id=2, replica_groups=mesh['dp'=8,'ctx'=4] {'ctx'}, dimensions={0}, use_global_device_ids=true | all-gather | bytes 5120 | tf_op jit(solution)/shard_map/all_gather | solution.py:8
  18.1 0.1 while.17
  18.3 0.2 divide_convert_fusion
  18.5 0.1 reshape.40
  18.6 4.1 %fusion.12 = bf16[4,8,4,2,1280]{4,1,3,2,0:T(8,128)(2,1)S(1)} fusion(bf16[4,640,1280]{2,1,0:T(8,128)(2,1)} %param.6, bf16[4,640,4,8,2]{1,4,3,2,0:T(2,128)(2,1)S(1)} %reshape.40), kind=kOutput, calls=%fused_computation.14 | convolution fusion | flops 419758080 | bytes 7536640 | tf_op jit(solution)/shard_map/ctabs,ctd->cbasd/dot_general | solution.py:58
  22.7 0.5 copy.30
  23.2 23.8 %all_to_all.10 = bf16[4,32,2,1280]{3,2,0,1:T(2,128)(2,1)S(1)} all-to-all(bf16[4,32,2,1280]{3,2,0,1:T(2,128)(2,1)S(1)} %bitcast.60), channel_id=1, replica_groups=mesh['dp'=8,'ctx'=4] {'dp','ctx'}, dimensions={1} | all-to-all | bytes 1310720 | tf_op jit(solution)/shard_map/all_to_all | solution.py:62
  47.0 0.7 bitcast_reduce_fusion
  47.7 0.1 copy.26
  47.8 0.1 convert_element_type.40
  47.9 8.0 %fusion.15 = bf16[64,1280]{1,0:T(8,128)(2,1)S(1)} fusion(bf16[1,2560,1280]{2,1,0:T(8,128)(2,1)} %param.9, bf16[64,1280]{1,0:T(8,128)(2,1)S(1)} %convert_element_type.40, bf16[1,1280,2560]{2,1,0:T(8,128)(2,1)} %param.8), kind=kOutput, calls=%fused_computation.15 | convolution fusion | flops 849592320 | bytes 13434880 | tf_op jit(solution)/shard_map/dot_general | solution.py:31
  55.9 0.1 reshape.44
  56.0 0.8 copy.27
  56.8 3.4 %all-to-all-start.1 = ((bf16[4,8,2,1280]{3,2,0,1:T(2,128)(2,1)}), bf16[4,8,2,1280]{3,2,0,1:T(2,128)(2,1)S(1)}, u32[]{:S(2)}, u32[]{:S(2)}) async-start(bf16[4,8,2,1280]{3,2,0,1:T(2,128)(2,1)} %copy.27), calls=%async_computation.1 | async-start | bytes 327680 | tf_op jit(solution)/shard_map/all_to_all | solution.py:66
  60.2 0.2 fusion.99
  60.3 7.7 %all-to-all-done.1 = bf16[4,8,2,1280]{3,2,0,1:T(2,128)(2,1)S(1)} async-done(((bf16[4,8,2,1280]{3,2,0,1:T(2,128)(2,1)}), bf16[4,8,2,1280]{3,2,0,1:T(2,128)(2,1)S(1)}, u32[]{:S(2)}, u32[]{:S(2)}) %all-to-all-start.1) | async-done | bytes 163872 | tf_op jit(solution)/shard_map/all_to_all | solution.py:66
  68.1 0.1 copy.28
  68.2 0.1 reshape.45
  68.3 7.9 %all_gather.19 = bf16[4,64,1280]{2,1,0:T(8,128)(2,1)S(1)} all-gather(bf16[4,16,1280]{2,1,0:T(8,128)(2,1)S(1)} %reshape.45), channel_id=1, replica_groups=mesh['dp'=8,'ctx'=4] {'ctx'}, dimensions={1}, use_global_device_ids=true | all-gather | bytes 819200 | tf_op jit(solution)/shard_map/all_gather | solution.py:71
  76.2 4.7 %convolution_convert_fusion = bf16[4,640,1280]{2,1,0:T(8,128)(2,1)} fusion(bf16[4,64,1280]{2,1,0:T(8,128)(2,1)S(1)} %all_gather.19, f32[4,640]{1,0:T(4,128)S(1)} %fusion.99, f32[4,640,64]{1,2,0:T(8,128)S(1)} %get-tuple-element.153), kind=kOutput, calls=%fused_computation.12 | convolution fusion | flops 423201344 | bytes 7874560 | tf_op jit(solution)/shard_map/ctj,cjd->ctd/dot_general | solution.py:68
  (6 shorter events, 0.1 us)
Async XLA Ops:
  56.8 11.3 %all-to-all-start.1 = ((bf16[4,8,2,1280]{3,2,0,1:T(2,128)(2,1)}), bf16[4,8,2,1280]{3,2,0,1:T(2,128)(2,1)S(1)}, u32[]{:S(2)}, u32[]{:S(2)}) async-start(bf16[4,8,2,1280]{3,2,0,1:T(2,128)(2,1)} %copy.27), calls=%async_computation.1 | async-start | bytes 327680 | tf_op jit(solution)/shard_map/all_to_all | solution.py:66
where the time goes:
time: 81.2 us; the launch traced here: 80.9 us
  blocking collectives  43.4 us (53%)
  matrix products  21.8 us (27%)
  waiting for transfers between devices  7.72 us (10%)
  starting transfers between devices  3.42 us (4%)
  local copies, waits for them, and re-layouts  3 us (4%)
  other arithmetic  1.36 us (2%)
    all_to_all x1, blocking collectives, shards(): lax.all_to_all(grouped, ('dp', 'ctx'), split_axis=1, concat_axis=1, tiled...  23.8 us
    all_gather x2, blocking collectives, merged(): everything = jax.tree.map(lambda part: lax.all_gather(part, axis), x)  11.7 us
    dot_general x1, matrix products, expert_rows(): jnp.dot(hidden, down_matrix, preferred_element_type=jnp.float32)  8.01 us
    all_gather x1, blocking collectives, shards(): lax.all_gather(returned, 'ctx', axis=1, tiled=True)  7.9 us
    all_to_all x1, waiting for transfers between devices, shards(): lax.all_to_all(results, 'dp', split_axis=1, concat_axis=1, tiled=True)  7.72 us
    dot_general x1, matrix products, shards(): jnp.einsum('ctd,dj->ctj', tokens, ordered, preferred_element_type=jnp.flo...  5.03 us
    dot_general x1, matrix products, shards(): jnp.einsum('ctj,cjd->ctd', combine, lax.all_gather(returned, 'ctx', axis=...  4.72 us
    dot_general x1, matrix products, shards(): jnp.einsum('ctabs,ctd->cbasd', split_dispatch, tokens, preferred_element_...  4.08 us
  transfers between devices with their start and end apart: 1, of which 1 were waited for; matrix products, arithmetic and copies ran while one was open for 0% of the time, Pallas kernels for 0%

commit v1 on v0

--- a/solution.py
+++ b/solution.py
@@ -2,6 +2,19 @@
 import jax.numpy as jnp
 from jax import lax
 from jax.sharding import PartitionSpec as P
+from jax.lax import axis_index, ppermute, psum
+
+
+def search_the_layers_all(arr, body):
+    b_next, mat_out, spare = (psum(1, "ctx"), axis_index("ctx"), arr.shape[1])
+    rack = [(pp, (pp + 1) % b_next) for pp in range(b_next)]
+    latest, carry_in = (arr, None)
+    for d in range(b_next):
+        even = ppermute(latest, "ctx", rack) if d < b_next - 1 else None
+        v_next = body(latest, (mat_out - d) % b_next * spare)
+        carry_in = v_next if carry_in is None else carry_in + v_next
+        latest = even
+    return carry_in
 
 
 def merged(x, axis, combine):
@@ -65,11 +78,14 @@
     results = expert_rows(jnp.sum(blocks, axis=2).astype(jnp.bfloat16), up_matrix, down_matrix)
     returned = lax.all_to_all(results, "dp", split_axis=1, concat_axis=1, tiled=True)
     returned = returned.reshape(clip_dev, dp_size * per_expert, feature)
-    mixed = jnp.einsum(
-        "ctj,cjd->ctd",
-        combine,
-        lax.all_gather(returned, "ctx", axis=1, tiled=True),
-        preferred_element_type=jnp.float32,
+    mixed = search_the_layers_all(
+        returned,
+        lambda own_block, at: jnp.einsum(
+            "ctj,cjd->ctd",
+            lax.dynamic_slice_in_dim(combine, at, own_block.shape[1], axis=2),
+            own_block,
+            preferred_element_type=jnp.float32,
+        ),
     )
     return mixed.astype(jnp.bfloat16)
 

time: 81.2 us -> 106 us (1.31)
  matrix products: 21.8 us -> 53.1 us
  blocking collectives: 43.4 us -> 35.5 us
  starting transfers between devices: 3.42 us -> 5.1 us
    dot_general x1 -> x4, matrix products: 4.72 us -> 36 us  [shards(): jnp.einsum('ctj,cjd->ctd', lax.dynamic_slice_in_dim(combine, at, own_bloc...]
    all_gather x1 -> x0, blocking collectives: 7.9 us -> none  [shards(): lax.all_gather(returned, 'ctx', axis=1, tiled=True)]
    ppermute x0 -> x3, starting transfers between devices: none -> 1.68 us  [search_the_layers_all(): even = ppermute(latest, 'ctx', rack) if d < b_next - 1 else None]
  transfers between devices with their start and end apart: 1 -> 4, of which waited for: 1 -> 1; matrix products, arithmetic and copies ran while one was open for 0% -> 20% of each run, Pallas kernels for 0% -> 0%
where the time goes in v1:
time: 106 us
  matrix products  53.1 us (50%)
  blocking collectives  35.5 us (33%)
  waiting for transfers between devices  6.69 us (6%)
  starting transfers between devices  5.1 us (5%)
  local copies, waits for them, and re-layouts  3 us (3%)
  other arithmetic  2.31 us (2%)
    dot_general x4, matrix products, shards(): jnp.einsum('ctj,cjd->ctd', lax.dynamic_slice_in_dim(combine, at, own_bloc...  36 us
    all_to_all x1, blocking collectives, shards(): lax.all_to_all(grouped, ('dp', 'ctx'), split_axis=1, concat_axis=1, tiled...  23.8 us
    all_gather x2, blocking collectives, merged(): everything = jax.tree.map(lambda part: lax.all_gather(part, axis), x)  11.7 us
    dot_general x1, matrix products, expert_rows(): jnp.dot(hidden, down_matrix, preferred_element_type=jnp.float32)  8.01 us
    all_to_all x1, waiting for transfers between devices, shards(): lax.all_to_all(results, 'dp', split_axis=1, concat_axis=1, tiled=True)  6.68 us
    dot_general x1, matrix products, shards(): jnp.einsum('ctd,dj->ctj', tokens, ordered, preferred_element_type=jnp.flo...  5.02 us
    dot_general x1, matrix products, shards(): jnp.einsum('ctabs,ctd->cbasd', split_dispatch, tokens, preferred_element_...  4.08 us
    all_to_all x1, starting transfers between devices, shards(): lax.all_to_all(results, 'dp', split_axis=1, concat_axis=1, tiled=True)  3.42 us
  transfers between devices with their start and end apart: 4, of which 1 were waited for; matrix products, arithmetic and copies ran while one was open for 20% of the time, Pallas kernels for 0%

profile of v1, /device:TPU:0, one launch (start us, length us, event | category | flops | bytes accessed | tf_op | source)
XLA Modules:
  0.0 106.0 jit_solution(17280990405096737258)
XLA Ops:
  0.0 1.0 reshape.38
  1.0 0.1 copy.22
  1.1 0.1 reshape.60
  1.2 5.0 %fusion.107 = (f32[4,64]{1,0:T(4,128)S(1)}, f32[4,640,64]{1,2,0:T(8,128)S(1)}) fusion(bf16[4,640,1280]{2,1,0:T(8,128)(2,1)} %param.6, bf16[1280,64,1]{0,1,2:T(8,128)(2,1)S(1)} %reshape.60), kind=kOutput, calls=%fused_computation.117 | convolution fusion | flops 419593984 | bytes 7373824 | tf_op jit(solution)/shard_map/ctd,dj->ctj/dot_general | solution.py:59
  6.2 0.3 fusion.34
  6.5 6.2 %all-gather.3 = f32[4,4,64]{2,1,0:T(4,128)S(1)} all-gather(f32[1,4,64]{2,1,0:T(4,128)S(1)} %bitcast.65), channel_id=3, replica_groups=mesh['dp'=8,'ctx'=4] {'ctx'}, dimensions={0}, use_global_device_ids=true | all-gather | bytes 5120 | tf_op jit(solution)/shard_map/all_gather | solution.py:21
  12.7 5.5 %all-gather.2 = f32[4,4,64]{2,1,0:T(4,128)S(1)} all-gather(f32[1,4,64]{2,1,0:T(4,128)S(1)} %bitcast.64), channel_id=2, replica_groups=mesh['dp'=8,'ctx'=4] {'ctx'}, dimensions={0}, use_global_device_ids=true | all-gather | bytes 5120 | tf_op jit(solution)/shard_map/all_gather | solution.py:21
  18.1 0.1 while.17
  18.2 0.2 divide_convert_fusion
  18.5 0.1 reshape.40
  18.6 4.1 %fusion.12 = bf16[4,8,4,2,1280]{4,1,3,2,0:T(8,128)(2,1)S(1)} fusion(bf16[4,640,1280]{2,1,0:T(8,128)(2,1)} %param.6, bf16[4,640,4,8,2]{1,4,3,2,0:T(2,128)(2,1)S(1)} %reshape.40), kind=kOutput, calls=%fused_computation.14 | convolution fusion | flops 419758080 | bytes 7536640 | tf_op jit(solution)/shard_map/ctabs,ctd->cbasd/dot_general | solution.py:71
  22.7 0.5 copy.30
  23.2 23.8 %all_to_all.10 = bf16[4,32,2,1280]{3,2,0,1:T(2,128)(2,1)S(1)} all-to-all(bf16[4,32,2,1280]{3,2,0,1:T(2,128)(2,1)S(1)} %bitcast.62), channel_id=1, replica_groups=mesh['dp'=8,'ctx'=4] {'dp','ctx'}, dimensions={1} | all-to-all | bytes 1310720 | tf_op jit(solution)/shard_map/all_to_all | solution.py:75
  47.0 0.7 bitcast_reduce_fusion
  47.7 0.1 copy.26
  47.8 0.1 convert_element_type.40
  47.9 8.0 %fusion.15 = bf16[64,1280]{1,0:T(8,128)(2,1)S(1)} fusion(bf16[1,2560,1280]{2,1,0:T(8,128)(2,1)} %param.9, bf16[64,1280]{1,0:T(8,128)(2,1)S(1)} %convert_element_type.40, bf16[1,1280,2560]{2,1,0:T(8,128)(2,1)} %param.8), kind=kOutput, calls=%fused_computation.15 | convolution fusion | flops 849592320 | bytes 13434880 | tf_op jit(solution)/shard_map/dot_general | solution.py:44
  55.9 0.1 reshape.44
  56.0 0.8 copy.27
  56.8 3.4 %all-to-all-start.1 = ((bf16[4,8,2,1280]{3,2,0,1:T(2,128)(2,1)}), bf16[4,8,2,1280]{3,2,0,1:T(2,128)(2,1)S(1)}, u32[]{:S(2)}, u32[]{:S(2)}) async-start(bf16[4,8,2,1280]{3,2,0,1:T(2,128)(2,1)} %copy.27), calls=%async_computation.1 | async-start | bytes 327680 | tf_op jit(solution)/shard_map/all_to_all | solution.py:79
  60.2 1.0 fusion.108
  61.3 0.1 divide_convert_fusion.1
  61.4 6.7 %all-to-all-done.1 = bf16[4,8,2,1280]{3,2,0,1:T(2,128)(2,1)S(1)} async-done(((bf16[4,8,2,1280]{3,2,0,1:T(2,128)(2,1)}), bf16[4,8,2,1280]{3,2,0,1:T(2,128)(2,1)S(1)}, u32[]{:S(2)}, u32[]{:S(2)}) %all-to-all-start.1) | async-done | bytes 163872 | tf_op jit(solution)/shard_map/all_to_all | solution.py:79
  68.1 0.1 copy.28
  68.2 0.1 reshape.45
  68.2 0.1 collective-permute-start
  68.3 6.6 %fusion.71 = f32[4,640,1280]{2,1,0:T(8,128)} fusion(bf16[4,16,1280]{2,1,0:T(8,128)(2,1)S(1)} %reshape.45, bf16[4,640,64]{1,2,0:T(8,128)(2,1)S(1)} %divide_convert_fusion.1, s32[]{:T(128)S(6)} %select_n.43), kind=kOutput, calls=%fused_computation.78 | convolution fusion | flops 104857600 | bytes 13352964 | tf_op jit(solution)/shard_map/ctj,cjd->ctd/dot_general | solution.py:83
  74.9 0.0 collective-permute-done
  74.9 1.6 %collective-permute-start.1 = (bf16[4,16,1280]{2,1,0:T(8,128)(2,1)S(1)}, bf16[4,16,1280]{2,1,0:T(8,128)(2,1)S(1)}, u32[]{:S(2)}, u32[]{:S(2)}) collective-permute-start(bf16[4,16,1280]{2,1,0:T(8,128)(2,1)S(1)} %collective-permute-done), channel_id=1, source_target_pairs={{0,1},{1,2},{2,3},{3,0},{4,5},{5,6},{6,7},{7,4},{8,9},{9,10},{10,1... | collective-permute-start | bytes 491528 | tf_op jit(solution)/shard_map/ppermute | solution.py:13
  76.5 6.6 %fusion.69 = f32[4,640,1280]{2,1,0:T(8,128)} fusion(bf16[4,16,1280]{2,1,0:T(8,128)(2,1)S(1)} %collective-permute-done, bf16[4,640,64]{1,2,0:T(8,128)(2,1)S(1)} %divide_convert_fusion.1, s32[]{:T(128)S(6)} %select_n.45), kind=kOutput, calls=%fused_computation.76 | convolution fusion | flops 104857600 | bytes 13352964 | tf_op jit(solution)/shard_map/ctj,cjd->ctd/dot_general | solution.py:83
  83.2 0.0 collective-permute-done.1
  83.2 0.0 collective-permute-start.2
  83.2 6.6 %fusion.67 = f32[4,640,1280]{2,1,0:T(8,128)} fusion(bf16[4,16,1280]{2,1,0:T(8,128)(2,1)S(1)} %collective-permute-done.1, bf16[4,640,64]{1,2,0:T(8,128)(2,1)S(1)} %divide_convert_fusion.1, s32[]{:T(128)S(6)} %select_n.47), kind=kOutput, calls=%fused_computation.74 | convolution fusion | flops 104857600 | bytes 13352964 | tf_op jit(solution)/shard_map/ctj,cjd->ctd/dot_general | solution.py:83
  89.8 0.0 collective-permute-done.2
  89.8 16.2 %add_convert_fusion = bf16[4,640,1280]{2,1,0:T(8,128)(2,1)} fusion(f32[4,640,1280]{2,1,0:T(8,128)} %fusion.67, f32[4,640,1280]{2,1,0:T(8,128)} %fusion.71, f32[4,640,1280]{2,1,0:T(8,128)} %fusion.69, bf16[4,16,1280]{2,1,0:T(8,128)(2,1)S(1)} %collective-permute-done.2, bf16[4,640,64]{1,2,0:T(8,128)(2,1)S(1)} %divide_convert_fusion.1, s32[]{:T(128)S(6)} %select_n.49), kind=kOutput, calls=%fused_computation.6 | convolution fusion | flops 117964800 | bytes 46120964 | tf_op jit(solution)/shard_map/ctj,cjd->ctd/dot_general | solution.py:83
  (6 shorter events, 0.1 us)
Async XLA Ops:
  56.8 11.3 %all-to-all-start.1 = ((bf16[4,8,2,1280]{3,2,0,1:T(2,128)(2,1)}), bf16[4,8,2,1280]{3,2,0,1:T(2,128)(2,1)S(1)}, u32[]{:S(2)}, u32[]{:S(2)}) async-start(bf16[4,8,2,1280]{3,2,0,1:T(2,128)(2,1)} %copy.27), calls=%async_computation.1 | async-start | bytes 327680 | tf_op jit(solution)/shard_map/all_to_all | solution.py:79
  68.2 6.7 %collective-permute-start = (bf16[4,16,1280]{2,1,0:T(8,128)(2,1)S(1)}, bf16[4,16,1280]{2,1,0:T(8,128)(2,1)S(1)}, u32[]{:S(2)}, u32[]{:S(2)}) collective-permute-start(bf16[4,16,1280]{2,1,0:T(8,128)(2,1)S(1)} %reshape.45), channel_id=1, source_target_pairs={{0,1},{1,2},{2,3},{3,0},{4,5},{5,6},{6,7},{7,4},{8,9},{9,10},{10,1... | collective-permute-start | bytes 491528 | tf_op jit(solution)/shard_map/ppermute | solution.py:13
  74.9 8.2 %collective-permute-start.1 = (bf16[4,16,1280]{2,1,0:T(8,128)(2,1)S(1)}, bf16[4,16,1280]{2,1,0:T(8,128)(2,1)S(1)}, u32[]{:S(2)}, u32[]{:S(2)}) collective-permute-start(bf16[4,16,1280]{2,1,0:T(8,128)(2,1)S(1)} %collective-permute-done), channel_id=1, source_target_pairs={{0,1},{1,2},{2,3},{3,0},{4,5},{5,6},{6,7},{7,4},{8,9},{9,10},{10,1... | collective-permute-start | bytes 491528 | tf_op jit(solution)/shard_map/ppermute | solution.py:13
  83.2 6.6 %collective-permute-start.2 = (bf16[4,16,1280]{2,1,0:T(8,128)(2,1)S(1)}, bf16[4,16,1280]{2,1,0:T(8,128)(2,1)S(1)}, u32[]{:S(2)}, u32[]{:S(2)}) collective-permute-start(bf16[4,16,1280]{2,1,0:T(8,128)(2,1)S(1)} %collective-permute-done.1), channel_id=1, source_target_pairs={{0,1},{1,2},{2,3},{3,0},{4,5},{5,6},{6,7},{7,4},{8,9},{9,10},{10,1... | collective-permute-start | bytes 491528 | tf_op jit(solution)/shard_map/ppermute | solution.py:13
